TPU v7x, 32 devices: a whole 2x2x4 slice. The times are simulated.
32 devices in a mesh: tm: 4 (over y, core), dom: 8 (over z, x).
Axes of the slice: x: 2, y: 2, z: 4, core: 2. Of those that a mesh axis runs over, the one named last changes fastest.
Arguments:
- particles: float32 [4, 64, 4096], P('tm', None, 'dom'), may hold values from -12 to 12, as said below
- noise: float32 [4, 64, 4096], P('tm', None, 'dom'), may hold values from -6 to 6
Outputs:
- advanced: float32 [4, 64, 4096], P('tm', None, 'dom')
Inputs may be any that keep to these rules, and one draw needn't show every extreme that they name: `particles`: positions of cells in principal components, each time point about a shifted centre.
All inputs are finite; a program needn't handle non-finite values.
Results may differ from a plain program's by a relative error of at most 0.012.
The roundings to bfloat16 on the way count: a program that leaves them out, or rounds other values in their place, can miss the bound.
Values may be sent and summed in bfloat16 or wider, within the bound.
A program may use at most 64 MiB of HBM per device.

v0:
```python
import math
import jax
import jax.numpy as jnp
from jax import lax
from jax.sharding import PartitionSpec as P

SWEEPS = 2
EPS = 4.0
STEP = 0.5
TEMP = 0.05


def passed_along(value, axis, steps):
    count = lax.axis_size(axis)
    leading, last = (max(0, -steps), min(count, count - steps))
    return lax.ppermute(value, axis, [(source, source + steps) for source in range(leading, last)])


def col_tiles(targets, potential):
    features = targets.shape[0]
    col_count = targets.shape[1]
    tile_width = math.gcd(col_count, 1024)
    tile_count = col_count // tile_width
    tiles = targets.reshape(features, tile_count, tile_width).transpose(1, 0, 2)
    return (tiles, potential.reshape(tile_count, tile_width))


def tile_scores(sources, target_tile, pot_tile):
    products = lax.dot_general(
        sources, target_tile, (((0,), (0,)), ((), ())), preferred_element_type=jnp.float32
    )
    return (products + pot_tile[None, :]) / EPS


def log_totals(sources, tiles, pot_tiles):
    row_count = sources.shape[1]

    def log_advance(carry, pieces):
        highest, totals = carry
        scores = tile_scores(sources, pieces[0], pieces[1])
        merged = jnp.maximum(highest, jnp.max(scores, axis=1))
        totals = totals * jnp.exp(highest - merged) + jnp.sum(
            jnp.exp(scores - merged[:, None]), axis=1
        )
        return ((merged, totals), None)

    start = (jnp.full((row_count,), -jnp.inf, jnp.float32), jnp.zeros((row_count,), jnp.float32))
    (highest, totals), unused = lax.scan(log_advance, start, (tiles, pot_tiles))
    return (highest, totals)


def update(sources, targets, potential):
    tiles, pot_tiles = col_tiles(targets, potential)
    highest, totals = log_totals(sources, tiles, pot_tiles)
    result = -EPS * (highest + jnp.log(totals)) + EPS * math.log(targets.shape[1])
    return (result, highest, totals)


def barycentre(sources, targets, potential, highest, totals):
    tiles, pot_tiles = col_tiles(targets, potential)

    def barycentre_advance(summed, pieces):
        scores = tile_scores(sources, pieces[0], pieces[1])
        weights = (jnp.exp(scores - highest[:, None]) / totals[:, None]).astype(jnp.bfloat16)
        summed = summed + lax.dot_general(
            pieces[0], weights, (((1,), (1,)), ((), ())), preferred_element_type=jnp.float32
        )
        return (summed, None)

    start = jnp.zeros((targets.shape[0], sources.shape[1]), jnp.float32)
    summed, unused = lax.scan(barycentre_advance, start, (tiles, pot_tiles))
    return summed


def neighbours(own_block):
    gathered = lax.all_gather(own_block, "dom", axis=1, tiled=True)
    next_all = passed_along(gathered, "tm", -1)
    prev_all = passed_along(gathered, "tm", 1)
    return (next_all, prev_all)


def potentials_from(values, offset):
    gathered = lax.all_gather(values, "dom", axis=0, tiled=True)
    return passed_along(gathered, "tm", offset)


def per_device(particles, noise):
    points = particles[0]
    rounded = points.astype(jnp.bfloat16)
    next_all, prev_all = neighbours(rounded)
    time_index = lax.axis_index("tm")
    last_time = lax.axis_size("tm") - 1
    next_pot = -0.5 * jnp.sum(jnp.square(next_all.astype(jnp.float32)), axis=0)
    for sweep_index in range(SWEEPS):
        if sweep_index > 0:
            next_pot = potentials_from(target_pot, -1)
        source_pot, unused_high, unused_totals = update(rounded, next_all, next_pot)
        prev_pot = potentials_from(source_pot, 1)
        target_pot, prev_high, prev_totals = update(rounded, prev_all, prev_pot)
    next_pot = potentials_from(target_pot, -1)
    next_tiles, next_pot_tiles = col_tiles(next_all, next_pot)
    next_high, next_totals = log_totals(rounded, next_tiles, next_pot_tiles)
    bary_next = barycentre(rounded, next_all, next_pot, next_high, next_totals)
    bary_prev = barycentre(rounded, prev_all, prev_pot, prev_high, prev_totals)
    pull_next = jnp.where(time_index < last_time, points - bary_next, 0.0)
    pull_prev = jnp.where(time_index > 0, points - bary_prev, 0.0)
    advanced = points - STEP * (pull_next + pull_prev) + math.sqrt(2.0 * STEP * TEMP) * noise[0]
    return advanced[None]


def solution(mesh):
    in_specs = (P("tm", None, "dom"), P("tm", None, "dom"))
    out_specs = P("tm", None, "dom")
    return jax.shard_map(
        per_device, mesh=mesh, in_specs=in_specs, out_specs=out_specs, check_vma=False
    )
```

profile of v0, /device:TPU:5, one launch (start us, length us, event | category | flops | bytes accessed | tf_op | source)
XLA Modules:
  0.0 191.1 jit_solution(3282749936282625119)
XLA Ops:
  0.0 0.9 bitcast_convert_fusion
  0.9 26.1 %all_gather.15 = bf16[64,4096]{1,0:T(8,128)(2,1)S(1)} all-gather(bf16[64,512]{1,0:T(8,128)(2,1)S(1)} %bitcast_convert_fusion), channel_id=1, replica_groups=mesh['tm'=4,'dom'=8] {'dom'}, dimensions={1}, use_global_device_ids=true | all-gather | bytes 589824 | tf_op jit(solution)/shard_map/all_gather | solution.py:76
  27.0 8.0 %collective-permute-start = (bf16[64,4096]{1,0:T(8,128)(2,1)S(1)}, bf16[64,4096]{1,0:T(8,128)(2,1)S(1)}, u32[]{:S(2)}, u32[]{:S(2)}) collective-permute-start(bf16[64,4096]{1,0:T(8,128)(2,1)S(1)} %all_gather.15), channel_id=1, source_target_pairs={{8,0},{16,8},{24,16},{9,1},{17,9},{25,17},{10,2},{18,10},{26,18},{... | collective-permute-start | bytes 1572872 | tf_op jit(solution)/shard_map/ppermute | solution.py:16
  35.1 1.3 collective-permute-start.1
  36.8 4.3 %while.87 = (s32[]{:T(128)}, f32[512]{0:T(512)S(1)}, f32[512]{0:T(512)S(1)}, bf16[4,64,1024]{2,1,0:T(8,128)(2,1)S(1)}, bf16[64,512]{1,0:T(8,128)(2,1)S(1)}, /*index=5*/f32[4,1024]{1,0:T(4,128)S(1)}, s32[]{:T(128)}, s32[]{:T(128)}) while((s32[]{:T(128)}, f32[512]{0:T(512)S(1)}, f32[512]{0:T(512)S(1)}, ...), condition=%wide.region_4.5_spmd.clone, body=%wide.region_1.4_spmd.clone.sunk | while | flops 70781440 | bytes 4434024 | solution.py:48
  41.1 21.5 %all-gather = f32[8,1,512]{2,1,0:T(1,128)S(1)} all-gather(f32[1,1,512]{2,1,0:T(1,128)S(1)} %bitcast.159), channel_id=1, replica_groups=mesh['tm'=4,'dom'=8] {'dom'}, dimensions={0}, use_global_device_ids=true | all-gather | bytes 18432 | tf_op jit(solution)/shard_map/all_gather | solution.py:83
  62.6 1.3 collective-permute-start.2
  63.9 1.1 copy.11
  65.0 9.9 %collective-permute-done.2 = f32[4096]{0:T(1024)S(1)} collective-permute-done((f32[4096]{0:T(1024)S(1)}, f32[4096]{0:T(1024)S(1)}, u32[]{:S(2)}, u32[]{:S(2)}) %collective-permute-start.2) | collective-permute-done | bytes 16416 | tf_op jit(solution)/shard_map/ppermute | solution.py:16
  75.0 4.3 %while.88 = (s32[]{:T(128)}, f32[512]{0:T(512)S(1)}, f32[512]{0:T(512)S(1)}, bf16[4,64,1024]{2,1,0:T(8,128)(2,1)S(1)}, bf16[64,512]{1,0:T(8,128)(2,1)S(1)}, /*index=5*/f32[4,1024]{1,0:T(4,128)S(1)}, s32[]{:T(128)}, s32[]{:T(128)}) while((s32[]{:T(128)}, f32[512]{0:T(512)S(1)}, f32[512]{0:T(512)S(1)}, ...), condition=%wide.region_8.9_spmd.clone, body=%wide.region_5.8_spmd.clone.sunk | while | flops 70781440 | bytes 4434024 | solution.py:48
  79.3 21.5 %all-gather.1 = f32[8,1,512]{2,1,0:T(1,128)S(1)} all-gather(f32[1,1,512]{2,1,0:T(1,128)S(1)} %bitcast.160), channel_id=1, replica_groups=mesh['tm'=4,'dom'=8] {'dom'}, dimensions={0}, use_global_device_ids=true | all-gather | bytes 18432 | tf_op jit(solution)/shard_map/all_gather | solution.py:83
  100.8 9.0 %collective-permute-start.3 = (f32[4096]{0:T(1024)S(1)}, f32[4096]{0:T(1024)S(1)}, u32[]{:S(2)}, u32[]{:S(2)}) collective-permute-start(f32[4096]{0:T(1024)S(1)} %bitcast.158), channel_id=1, source_target_pairs={{8,0},{16,8},{24,16},{9,1},{17,9},{25,17},{10,2},{18,10},{26,18},{... | collective-permute-start | bytes 49160 | tf_op jit(solution)/shard_map/ppermute | solution.py:16
  110.6 4.3 %while.89 = (s32[]{:T(128)}, f32[512]{0:T(512)S(1)}, f32[512]{0:T(512)S(1)}, bf16[4,64,1024]{2,1,0:T(8,128)(2,1)S(1)}, bf16[64,512]{1,0:T(8,128)(2,1)S(1)}, /*index=5*/f32[4,1024]{1,0:T(4,128)S(1)}, s32[]{:T(128)}, s32[]{:T(128)}) while((s32[]{:T(128)}, f32[512]{0:T(512)S(1)}, f32[512]{0:T(512)S(1)}, ...), condition=%wide.region_12.13_spmd.clone, body=%wide.region_9.12_spmd.clone.sunk | while | flops 70781440 | bytes 4434024 | solution.py:48
  114.9 21.5 %all-gather.2 = f32[8,1,512]{2,1,0:T(1,128)S(1)} all-gather(f32[1,1,512]{2,1,0:T(1,128)S(1)} %bitcast.161), channel_id=1, replica_groups=mesh['tm'=4,'dom'=8] {'dom'}, dimensions={0}, use_global_device_ids=true | all-gather | bytes 18432 | tf_op jit(solution)/shard_map/all_gather | solution.py:83
  136.4 1.3 collective-permute-start.4
  137.8 6.4 %collective-permute-done.4 = f32[4096]{0:T(1024)S(1)} collective-permute-done((f32[4096]{0:T(1024)S(1)}, f32[4096]{0:T(1024)S(1)}, u32[]{:S(2)}, u32[]{:S(2)}) %collective-permute-start.4) | collective-permute-done | bytes 16416 | tf_op jit(solution)/shard_map/ppermute | solution.py:16
  144.2 4.3 %while.90 = (s32[]{:T(128)}, f32[512]{0:T(512)S(1)}, f32[512]{0:T(512)S(1)}, bf16[4,64,1024]{2,1,0:T(8,128)(2,1)S(1)}, bf16[64,512]{1,0:T(8,128)(2,1)S(1)}, /*index=5*/f32[4,1024]{1,0:T(4,128)S(1)}, s32[]{:T(128)}, s32[]{:T(128)}) while((s32[]{:T(128)}, f32[512]{0:T(512)S(1)}, f32[512]{0:T(512)S(1)}, ...), condition=%wide.region_16.17_spmd.clone, body=%wide.region_13.16_spmd.clone.sunk | while | flops 70781440 | bytes 4434024 | solution.py:48
  148.5 21.5 %all-gather.3 = f32[8,1,512]{2,1,0:T(1,128)S(1)} all-gather(f32[1,1,512]{2,1,0:T(1,128)S(1)} %bitcast.162), channel_id=1, replica_groups=mesh['tm'=4,'dom'=8] {'dom'}, dimensions={0}, use_global_device_ids=true | all-gather | bytes 18432 | tf_op jit(solution)/shard_map/all_gather | solution.py:83
  170.0 9.0 %collective-permute-start.5 = (f32[4096]{0:T(1024)S(1)}, f32[4096]{0:T(1024)S(1)}, u32[]{:S(2)}, u32[]{:S(2)}) collective-permute-start(f32[4096]{0:T(1024)S(1)} %bitcast.155), channel_id=1, source_target_pairs={{8,0},{16,8},{24,16},{9,1},{17,9},{25,17},{10,2},{18,10},{26,18},{... | collective-permute-start | bytes 49160 | tf_op jit(solution)/shard_map/ppermute | solution.py:16
  179.0 3.5 %while.93 = (s32[]{:T(128)}, f32[64,512]{1,0:T(8,128)S(1)}, bf16[4,64,1024]{2,1,0:T(8,128)(2,1)S(1)}, bf16[64,512]{1,0:T(8,128)(2,1)S(1)}, f32[4,1024]{1,0:T(4,1...) while((s32[]{:T(128)}, f32[64,512]{1,0:T(8,128)S(1)}, ...), condition=%wide.region_24.25_spmd.clone, body=%wide.region_23.24_spmd.clone.sunk | while | flops 136904704 | bytes 607339 | solution.py:71
  179.9 0.8 fusion.113
  180.8 0.8 fusion.113
  182.6 4.3 %while.91 = (s32[]{:T(128)}, f32[512]{0:T(512)S(1)}, f32[512]{0:T(512)S(1)}, bf16[4,64,1024]{2,1,0:T(8,128)(2,1)S(1)}, bf16[64,512]{1,0:T(8,128)(2,1)S(1)}, /*index=5*/f32[4,1024]{1,0:T(4,128)S(1)}, s32[]{:T(128)}, s32[]{:T(128)}) while((s32[]{:T(128)}, f32[512]{0:T(512)S(1)}, f32[512]{0:T(512)S(1)}, ...), condition=%wide.region_20.21_spmd.clone, body=%wide.region_17.20_spmd.clone.sunk | while | flops 70781440 | bytes 4434024 | solution.py:48
  186.9 3.5 %while.92 = (s32[]{:T(128)}, f32[64,512]{1,0:T(8,128)S(1)}, bf16[4,64,1024]{2,1,0:T(8,128)(2,1)S(1)}, bf16[64,512]{1,0:T(8,128)(2,1)S(1)}, f32[4,1024]{1,0:T(4,1...) while((s32[]{:T(128)}, f32[64,512]{1,0:T(8,128)S(1)}, ...), condition=%wide.region_22.23_spmd.clone, body=%wide.region_21.22_spmd.clone.sunk | while | flops 136904704 | bytes 607339 | solution.py:71
  (167 shorter events, 27.5 us)
Async XLA Ops:
  27.0 9.5 %collective-permute-start = (bf16[64,4096]{1,0:T(8,128)(2,1)S(1)}, bf16[64,4096]{1,0:T(8,128)(2,1)S(1)}, u32[]{:S(2)}, u32[]{:S(2)}) collective-permute-start(bf16[64,4096]{1,0:T(8,128)(2,1)S(1)} %all_gather.15), channel_id=1, source_target_pairs={{8,0},{16,8},{24,16},{9,1},{17,9},{25,17},{10,2},{18,10},{26,18},{... | collective-permute-start | bytes 1572872 | tf_op jit(solution)/shard_map/ppermute | solution.py:16
  35.1 28.8 %collective-permute-start.1 = (bf16[64,4096]{1,0:T(8,128)(2,1)S(1)}, bf16[64,4096]{1,0:T(8,128)(2,1)}, u32[]{:S(2)}, u32[]{:S(2)}) collective-permute-start(bf16[64,4096]{1,0:T(8,128)(2,1)S(1)} %all_gather.15), channel_id=1, source_target_pairs={{0,8},{8,16},{16,24},{1,9},{9,17},{17,25},{2,10},{10,18},{18,26},{... | collective-permute-start | bytes 1572872 | tf_op jit(solution)/shard_map/ppermute | solution.py:16
  62.6 12.3 %collective-permute-start.2 = (f32[4096]{0:T(1024)S(1)}, f32[4096]{0:T(1024)S(1)}, u32[]{:S(2)}, u32[]{:S(2)}) collective-permute-start(f32[4096]{0:T(1024)S(1)} %bitcast.157), channel_id=1, source_target_pairs={{0,8},{8,16},{16,24},{1,9},{9,17},{17,25},{2,10},{10,18},{18,26},{... | collective-permute-start | bytes 49160 | tf_op jit(solution)/shard_map/ppermute | solution.py:16
  100.8 9.8 %collective-permute-start.3 = (f32[4096]{0:T(1024)S(1)}, f32[4096]{0:T(1024)S(1)}, u32[]{:S(2)}, u32[]{:S(2)}) collective-permute-start(f32[4096]{0:T(1024)S(1)} %bitcast.158), channel_id=1, source_target_pairs={{8,0},{16,8},{24,16},{9,1},{17,9},{25,17},{10,2},{18,10},{26,18},{... | collective-permute-start | bytes 49160 | tf_op jit(solution)/shard_map/ppermute | solution.py:16
  136.4 7.8 %collective-permute-start.4 = (f32[4096]{0:T(1024)S(1)}, f32[4096]{0:T(1024)S(1)}, u32[]{:S(2)}, u32[]{:S(2)}) collective-permute-start(f32[4096]{0:T(1024)S(1)} %bitcast.156), channel_id=1, source_target_pairs={{0,8},{8,16},{16,24},{1,9},{9,17},{17,25},{2,10},{10,18},{18,26},{... | collective-permute-start | bytes 49160 | tf_op jit(solution)/shard_map/ppermute | solution.py:16
  170.0 12.5 %collective-permute-start.5 = (f32[4096]{0:T(1024)S(1)}, f32[4096]{0:T(1024)S(1)}, u32[]{:S(2)}, u32[]{:S(2)}) collective-permute-start(f32[4096]{0:T(1024)S(1)} %bitcast.155), channel_id=1, source_target_pairs={{8,0},{16,8},{24,16},{9,1},{17,9},{25,17},{10,2},{18,10},{26,18},{... | collective-permute-start | bytes 49160 | tf_op jit(solution)/shard_map/ppermute | solution.py:16
  186.9 3.5 %copy-start = (f32[1,64,512]{2,1,0:T(8,128)S(1)}, f32[1,64,512]{2,1,0:T(8,128)}, u32[]{:S(2)}) copy-start(f32[1,64,512]{2,1,0:T(8,128)} %param.16) | copy-start | bytes 393220
  186.9 3.5 %copy-start.1 = (f32[1,64,512]{2,1,0:T(8,128)S(1)}, f32[1,64,512]{2,1,0:T(8,128)}, u32[]{:S(2)}) copy-start(f32[1,64,512]{2,1,0:T(8,128)} %param.17) | copy-start | bytes 393220
where the time goes:
time: 191 us
  blocking collectives  112 us (59%)
  starting transfers between devices  29.8 us (16%)
  waiting for transfers between devices  17.3 us (9%)
  matrix products  16.5 us (9%)
  other arithmetic  12.2 us (6%)
    all_gather x4, blocking collectives, potentials_from(): gathered = lax.all_gather(values, 'dom', axis=0, tiled=True)  86.1 us
    ppermute x6, starting transfers between devices, passed_along(): lax.ppermute(value, axis, [(source, source + steps) for source in range(l...  29.8 us
    all_gather x1, blocking collectives, neighbours(): gathered = lax.all_gather(own_block, 'dom', axis=1, tiled=True)  26.1 us
    ppermute x6, waiting for transfers between devices, passed_along(): lax.ppermute(value, axis, [(source, source + steps) for source in range(l...  17.3 us
    reduce_sum x20, other arithmetic, log_advance(): jnp.sum(jnp.exp(scores - merged[:, None]), axis=1)  9.89 us
    dot_general x20, matrix products, tile_scores(): lax.dot_general(sources, target_tile, (((0,), (0,)), ((), ())), preferred...  9.87 us
    dot_general x8, matrix products, barycentre_advance(): lax.dot_general(pieces[0], weights, (((1,), (1,)), ((), ())), preferred_e...  6.65 us
  transfers between devices with their start and end apart: 6, of which 4 were waited for; matrix products, arithmetic and copies ran while one was open for 5% of the time, Pallas kernels for 0%

commit v1 on v0

--- a/solution.py
+++ b/solution.py
@@ -80,7 +80,15 @@
 
 
 def potentials_from(values, offset):
-    gathered = lax.all_gather(values, "dom", axis=0, tiled=True)
+    ways, here = (lax.axis_size("dom"), lax.axis_index("dom"))
+    grown, reach = (values, 1)
+    while reach < ways:
+        theirs = lax.ppermute(grown, "dom", [(d, d ^ reach) for d in range(ways)])
+        mine_first = jnp.concatenate([grown, theirs], axis=0)
+        theirs_first = jnp.concatenate([theirs, grown], axis=0)
+        grown = jnp.where(here & reach == 0, mine_first, theirs_first)
+        reach = 2 * reach
+    gathered = grown
     return passed_along(gathered, "tm", offset)
 
 

time: 191 us -> 134 us (0.70)
  blocking collectives: 112 us -> 26.1 us
  waiting for transfers between devices: 17.3 us -> 34.9 us
  starting transfers between devices: 29.8 us -> 41.2 us
    all_gather x4 -> x0, blocking collectives: 86.1 us -> none  [potentials_from(): gathered = lax.all_gather(values, 'dom', axis=0, tiled=True)]
    ppermute x0 -> x12, waiting for transfers between devices: none -> 20.2 us  [potentials_from(): theirs = lax.ppermute(grown, 'dom', [(d, d ^ reach) for d in range(ways)])]
    ppermute x0 -> x12, starting transfers between devices: none -> 13.7 us  [potentials_from(): theirs = lax.ppermute(grown, 'dom', [(d, d ^ reach) for d in range(ways)])]
    ppermute x6, waiting for transfers between devices: 17.3 us -> 14.7 us  [passed_along(): lax.ppermute(value, axis, [(source, source + steps) for source in range(l...]
    ppermute x6, starting transfers between devices: 29.8 us -> 27.5 us  [passed_along(): lax.ppermute(value, axis, [(source, source + steps) for source in range(l...]
  transfers between devices with their start and end apart: 6 -> 18, of which waited for: 4 -> 16; matrix products, arithmetic and copies ran while one was open for 5% -> 7% of each run, Pallas kernels for 0% -> 0%
where the time goes in v1:
time: 134 us
  starting transfers between devices  41.2 us (31%)
  waiting for transfers between devices  34.9 us (26%)
  blocking collectives  26.1 us (19%)
  matrix products  16.5 us (12%)
  other arithmetic  12.2 us (9%)
  local copies, waits for them, and re-layouts  1.49 us (1%)
    ppermute x6, starting transfers between devices, passed_along(): lax.ppermute(value, axis, [(source, source + steps) for source in range(l...  27.5 us
    all_gather x1, blocking collectives, neighbours(): gathered = lax.all_gather(own_block, 'dom', axis=1, tiled=True)  26.1 us
    ppermute x12, waiting for transfers between devices, potentials_from(): theirs = lax.ppermute(grown, 'dom', [(d, d ^ reach) for d in range(ways)])  20.2 us
    ppermute x6, waiting for transfers between devices, passed_along(): lax.ppermute(value, axis, [(source, source + steps) for source in range(l...  14.7 us
    ppermute x12, starting transfers between devices, potentials_from(): theirs = lax.ppermute(grown, 'dom', [(d, d ^ reach) for d in range(ways)])  13.7 us
    reduce_sum x20, other arithmetic, log_advance(): jnp.sum(jnp.exp(scores - merged[:, None]), axis=1)  9.89 us
    dot_general x20, matrix products, tile_scores(): lax.dot_general(sources, target_tile, (((0,), (0,)), ((), ())), preferred...  9.88 us
    dot_general x8, matrix products, barycentre_advance(): lax.dot_general(pieces[0], weights, (((1,), (1,)), ((), ())), preferred_e...  6.65 us
  transfers between devices with their start and end apart: 18, of which 16 were waited for; matrix products, arithmetic and copies ran while one was open for 7% of the time, Pallas kernels for 0%

profile of v1, /device:TPU:5, one launch (start us, length us, event | category | flops | bytes accessed | tf_op | source)
XLA Modules:
  0.0 134.0 jit_solution(13025605784092336594)
XLA Ops:
  0.9 26.1 %all_gather.3 = bf16[64,4096]{1,0:T(8,128)(2,1)S(1)} all-gather(bf16[64,512]{1,0:T(8,128)(2,1)S(1)} %bitcast_convert_fusion), channel_id=1, replica_groups=mesh['tm'=4,'dom'=8] {'dom'}, dimensions={1}, use_global_device_ids=true | all-gather | bytes 589824 | tf_op jit(solution)/shard_map/all_gather | solution.py:76
  27.0 8.0 %collective-permute-start = (bf16[64,4096]{1,0:T(8,128)(2,1)S(1)}, bf16[64,4096]{1,0:T(8,128)(2,1)S(1)}, u32[]{:S(2)}, u32[]{:S(2)}) collective-permute-start(bf16[64,4096]{1,0:T(8,128)(2,1)S(1)} %all_gather.3), channel_id=1, source_target_pairs={{8,0},{16,8},{24,16},{9,1},{17,9},{25,17},{10,2},{18,10},{26,18},{... | collective-permute-start | bytes 1572872 | tf_op jit(solution)/shard_map/ppermute | solution.py:16
  36.8 4.3 %while.87 = (s32[]{:T(128)}, f32[512]{0:T(512)S(1)}, f32[512]{0:T(512)S(1)}, bf16[4,64,1024]{2,1,0:T(8,128)(2,1)S(1)}, bf16[64,512]{1,0:T(8,128)(2,1)S(1)}, /*index=5*/f32[4,1024]{1,0:T(4,128)S(1)}, s32[]{:T(128)}, s32[]{:T(128)}) while((s32[]{:T(128)}, f32[512]{0:T(512)S(1)}, f32[512]{0:T(512)S(1)}, ...), condition=%wide.region_4.5_spmd.clone, body=%wide.region_1.4_spmd.clone.sunk | while | flops 70781440 | bytes 4434024 | solution.py:48
  44.0 2.4 %collective-permute-done.3 = f32[1024]{0:T(1024)S(1)} collective-permute-done((f32[1024]{0:T(1024)S(1)}, f32[1024]{0:T(1024)S(1)}, u32[]{:S(2)}, u32[]{:S(2)}) %collective-permute-start.3) | collective-permute-done | bytes 4128 | tf_op jit(solution)/shard_map/ppermute | solution.py:86
  47.8 2.1 %collective-permute-done.4 = f32[2048]{0:T(1024)S(1)} collective-permute-done((f32[2048]{0:T(1024)S(1)}, f32[2048]{0:T(1024)S(1)}, u32[]{:S(2)}, u32[]{:S(2)}) %collective-permute-start.4) | collective-permute-done | bytes 8224 | tf_op jit(solution)/shard_map/ppermute | solution.py:86
  52.3 8.4 %collective-permute-done.5 = f32[4096]{0:T(1024)S(1)} collective-permute-done((f32[4096]{0:T(1024)S(1)}, f32[4096]{0:T(1024)S(1)}, u32[]{:S(2)}, u32[]{:S(2)}) %collective-permute-start.5) | collective-permute-done | bytes 16416 | tf_op jit(solution)/shard_map/ppermute | solution.py:16
  60.7 4.3 %while.88 = (s32[]{:T(128)}, f32[512]{0:T(512)S(1)}, f32[512]{0:T(512)S(1)}, bf16[4,64,1024]{2,1,0:T(8,128)(2,1)S(1)}, bf16[64,512]{1,0:T(8,128)(2,1)S(1)}, /*index=5*/f32[4,1024]{1,0:T(4,128)S(1)}, s32[]{:T(128)}, s32[]{:T(128)}) while((s32[]{:T(128)}, f32[512]{0:T(512)S(1)}, f32[512]{0:T(512)S(1)}, ...), condition=%wide.region_8.9_spmd.clone, body=%wide.region_5.8_spmd.clone.sunk | while | flops 70781440 | bytes 4434024 | solution.py:48
  68.0 2.0 %collective-permute-done.7 = f32[1024]{0:T(1024)S(1)} collective-permute-done((f32[1024]{0:T(1024)S(1)}, f32[1024]{0:T(1024)S(1)}, u32[]{:S(2)}, u32[]{:S(2)}) %collective-permute-start.7) | collective-permute-done | bytes 4128 | tf_op jit(solution)/shard_map/ppermute | solution.py:86
  70.0 1.9 %collective-permute-start.8 = (f32[2048]{0:T(1024)S(1)}, f32[2048]{0:T(1024)S(1)}, u32[]{:S(2)}, u32[]{:S(2)}) collective-permute-start(f32[2048]{0:T(1024)S(1)} %maximum_select_fusion.5), channel_id=1, source_target_pairs={{0,4},{1,5},{2,6},{3,7},{4,0},{5,1},{6,2},{7,3},{8,12},{9,13},{10,... | collective-permute-start | bytes 24584 | tf_op jit(solution)/shard_map/ppermute | solution.py:86
  71.9 1.5 %collective-permute-done.8 = f32[2048]{0:T(1024)S(1)} collective-permute-done((f32[2048]{0:T(1024)S(1)}, f32[2048]{0:T(1024)S(1)}, u32[]{:S(2)}, u32[]{:S(2)}) %collective-permute-start.8) | collective-permute-done | bytes 8224 | tf_op jit(solution)/shard_map/ppermute | solution.py:86
  73.4 7.8 %collective-permute-start.9 = (f32[4096]{0:T(1024)S(1)}, f32[4096]{0:T(1024)S(1)}, u32[]{:S(2)}, u32[]{:S(2)}) collective-permute-start(f32[4096]{0:T(1024)S(1)} %maximum_select_fusion.1), channel_id=1, source_target_pairs={{8,0},{16,8},{24,16},{9,1},{17,9},{25,17},{10,2},{18,10},{26,18},{... | collective-permute-start | bytes 49160 | tf_op jit(solution)/shard_map/ppermute | solution.py:16
  82.1 4.3 %while.89 = (s32[]{:T(128)}, f32[512]{0:T(512)S(1)}, f32[512]{0:T(512)S(1)}, bf16[4,64,1024]{2,1,0:T(8,128)(2,1)S(1)}, bf16[64,512]{1,0:T(8,128)(2,1)S(1)}, /*index=5*/f32[4,1024]{1,0:T(4,128)S(1)}, s32[]{:T(128)}, s32[]{:T(128)}) while((s32[]{:T(128)}, f32[512]{0:T(512)S(1)}, f32[512]{0:T(512)S(1)}, ...), condition=%wide.region_12.13_spmd.clone, body=%wide.region_9.12_spmd.clone.sunk | while | flops 70781440 | bytes 4434024 | solution.py:48
  89.4 2.0 %collective-permute-done.11 = f32[1024]{0:T(1024)S(1)} collective-permute-done((f32[1024]{0:T(1024)S(1)}, f32[1024]{0:T(1024)S(1)}, u32[]{:S(2)}, u32[]{:S(2)}) %collective-permute-start.11) | collective-permute-done | bytes 4128 | tf_op jit(solution)/shard_map/ppermute | solution.py:86
  91.4 1.6 %collective-permute-start.12 = (f32[2048]{0:T(1024)S(1)}, f32[2048]{0:T(1024)S(1)}, u32[]{:S(2)}, u32[]{:S(2)}) collective-permute-start(f32[2048]{0:T(1024)S(1)} %maximum_select_fusion.6), channel_id=1, source_target_pairs={{0,4},{1,5},{2,6},{3,7},{4,0},{5,1},{6,2},{7,3},{8,12},{9,13},{10,... | collective-permute-start | bytes 24584 | tf_op jit(solution)/shard_map/ppermute | solution.py:86
  93.0 1.8 %collective-permute-done.12 = f32[2048]{0:T(1024)S(1)} collective-permute-done((f32[2048]{0:T(1024)S(1)}, f32[2048]{0:T(1024)S(1)}, u32[]{:S(2)}, u32[]{:S(2)}) %collective-permute-start.12) | collective-permute-done | bytes 8224 | tf_op jit(solution)/shard_map/ppermute | solution.py:86
  96.1 5.3 %collective-permute-done.13 = f32[4096]{0:T(1024)S(1)} collective-permute-done((f32[4096]{0:T(1024)S(1)}, f32[4096]{0:T(1024)S(1)}, u32[]{:S(2)}, u32[]{:S(2)}) %collective-permute-start.13) | collective-permute-done | bytes 16416 | tf_op jit(solution)/shard_map/ppermute | solution.py:16
  101.4 4.3 %while.90 = (s32[]{:T(128)}, f32[512]{0:T(512)S(1)}, f32[512]{0:T(512)S(1)}, bf16[4,64,1024]{2,1,0:T(8,128)(2,1)S(1)}, bf16[64,512]{1,0:T(8,128)(2,1)S(1)}, /*index=5*/f32[4,1024]{1,0:T(4,128)S(1)}, s32[]{:T(128)}, s32[]{:T(128)}) while((s32[]{:T(128)}, f32[512]{0:T(512)S(1)}, f32[512]{0:T(512)S(1)}, ...), condition=%wide.region_16.17_spmd.clone, body=%wide.region_13.16_spmd.clone.sunk | while | flops 70781440 | bytes 4434024 | solution.py:48
  108.7 2.0 %collective-permute-done.15 = f32[1024]{0:T(1024)S(1)} collective-permute-done((f32[1024]{0:T(1024)S(1)}, f32[1024]{0:T(1024)S(1)}, u32[]{:S(2)}, u32[]{:S(2)}) %collective-permute-start.15) | collective-permute-done | bytes 4128 | tf_op jit(solution)/shard_map/ppermute | solution.py:86
  110.7 1.9 %collective-permute-start.16 = (f32[2048]{0:T(1024)S(1)}, f32[2048]{0:T(1024)S(1)}, u32[]{:S(2)}, u32[]{:S(2)}) collective-permute-start(f32[2048]{0:T(1024)S(1)} %maximum_select_fusion.7), channel_id=1, source_target_pairs={{0,4},{1,5},{2,6},{3,7},{4,0},{5,1},{6,2},{7,3},{8,12},{9,13},{10,... | collective-permute-start | bytes 24584 | tf_op jit(solution)/shard_map/ppermute | solution.py:86
  112.5 1.5 %collective-permute-done.16 = f32[2048]{0:T(1024)S(1)} collective-permute-done((f32[2048]{0:T(1024)S(1)}, f32[2048]{0:T(1024)S(1)}, u32[]{:S(2)}, u32[]{:S(2)}) %collective-permute-start.16) | collective-permute-done | bytes 8224 | tf_op jit(solution)/shard_map/ppermute | solution.py:86
  114.1 7.8 %collective-permute-start.17 = (f32[4096]{0:T(1024)S(1)}, f32[4096]{0:T(1024)S(1)}, u32[]{:S(2)}, u32[]{:S(2)}) collective-permute-start(f32[4096]{0:T(1024)S(1)} %maximum_select_fusion.3), channel_id=1, source_target_pairs={{8,0},{16,8},{24,16},{9,1},{17,9},{25,17},{10,2},{18,10},{26,18},{... | collective-permute-start | bytes 49160 | tf_op jit(solution)/shard_map/ppermute | solution.py:16
  121.9 3.5 %while.93 = (s32[]{:T(128)}, f32[64,512]{1,0:T(8,128)S(1)}, bf16[4,64,1024]{2,1,0:T(8,128)(2,1)S(1)}, bf16[64,512]{1,0:T(8,128)(2,1)S(1)}, f32[4,1024]{1,0:T(4,1...) while((s32[]{:T(128)}, f32[64,512]{1,0:T(8,128)S(1)}, ...), condition=%wide.region_24.25_spmd.clone, body=%wide.region_23.24_spmd.clone.sunk | while | flops 136904704 | bytes 607339 | solution.py:71
  125.5 4.3 %while.91 = (s32[]{:T(128)}, f32[512]{0:T(512)S(1)}, f32[512]{0:T(512)S(1)}, bf16[4,64,1024]{2,1,0:T(8,128)(2,1)S(1)}, bf16[64,512]{1,0:T(8,128)(2,1)S(1)}, /*index=5*/f32[4,1024]{1,0:T(4,128)S(1)}, s32[]{:T(128)}, s32[]{:T(128)}) while((s32[]{:T(128)}, f32[512]{0:T(512)S(1)}, f32[512]{0:T(512)S(1)}, ...), condition=%wide.region_20.21_spmd.clone, body=%wide.region_17.20_spmd.clone.sunk | while | flops 70781440 | bytes 4434024 | solution.py:48
  129.8 3.5 %while.92 = (s32[]{:T(128)}, f32[64,512]{1,0:T(8,128)S(1)}, bf16[4,64,1024]{2,1,0:T(8,128)(2,1)S(1)}, bf16[64,512]{1,0:T(8,128)(2,1)S(1)}, f32[4,1024]{1,0:T(4,1...) while((s32[]{:T(128)}, f32[64,512]{1,0:T(8,128)S(1)}, ...), condition=%wide.region_22.23_spmd.clone, body=%wide.region_21.22_spmd.clone.sunk | while | flops 136904704 | bytes 607339 | solution.py:71
  (199 shorter events, 48.2 us)
Async XLA Ops:
  27.0 9.5 %collective-permute-start = (bf16[64,4096]{1,0:T(8,128)(2,1)S(1)}, bf16[64,4096]{1,0:T(8,128)(2,1)S(1)}, u32[]{:S(2)}, u32[]{:S(2)}) collective-permute-start(bf16[64,4096]{1,0:T(8,128)(2,1)S(1)} %all_gather.3), channel_id=1, source_target_pairs={{8,0},{16,8},{24,16},{9,1},{17,9},{25,17},{10,2},{18,10},{26,18},{... | collective-permute-start | bytes 1572872 | tf_op jit(solution)/shard_map/ppermute | solution.py:16
  35.1 16.1 %collective-permute-start.1 = (bf16[64,4096]{1,0:T(8,128)(2,1)S(1)}, bf16[64,4096]{1,0:T(8,128)(2,1)}, u32[]{:S(2)}, u32[]{:S(2)}) collective-permute-start(bf16[64,4096]{1,0:T(8,128)(2,1)S(1)} %all_gather.3), channel_id=1, source_target_pairs={{0,8},{8,16},{16,24},{1,9},{9,17},{17,25},{2,10},{10,18},{18,26},{... | collective-permute-start | bytes 1572872 | tf_op jit(solution)/shard_map/ppermute | solution.py:16
  41.1 2.9 %collective-permute-start.2 = (f32[512]{0:T(512)S(1)}, f32[512]{0:T(512)S(1)}, u32[]{:S(2)}, u32[]{:S(2)}) collective-permute-start(f32[512]{0:T(512)S(1)} %multiply_add_fusion.3), channel_id=1, source_target_pairs={{0,1},{1,0},{2,3},{3,2},{4,5},{5,4},{6,7},{7,6},{8,9},{9,8},{10,11... | collective-permute-start | bytes 6152 | tf_op jit(solution)/shard_map/ppermute | solution.py:86
  44.0 2.5 %collective-permute-start.3 = (f32[1024]{0:T(1024)S(1)}, f32[1024]{0:T(1024)S(1)}, u32[]{:S(2)}, u32[]{:S(2)}) collective-permute-start(f32[1024]{0:T(1024)S(1)} %maximum_select_fusion.8), channel_id=1, source_target_pairs={{0,2},{1,3},{2,0},{3,1},{4,6},{5,7},{6,4},{7,5},{8,10},{9,11},{10,... | collective-permute-start | bytes 12296 | tf_op jit(solution)/shard_map/ppermute | solution.py:86
  46.5 3.4 %collective-permute-start.4 = (f32[2048]{0:T(1024)S(1)}, f32[2048]{0:T(1024)S(1)}, u32[]{:S(2)}, u32[]{:S(2)}) collective-permute-start(f32[2048]{0:T(1024)S(1)} %maximum_select_fusion.4), channel_id=1, source_target_pairs={{0,4},{1,5},{2,6},{3,7},{4,0},{5,1},{6,2},{7,3},{8,12},{9,13},{10,... | collective-permute-start | bytes 24584 | tf_op jit(solution)/shard_map/ppermute | solution.py:86
  49.9 10.8 %collective-permute-start.5 = (f32[4096]{0:T(1024)S(1)}, f32[4096]{0:T(1024)S(1)}, u32[]{:S(2)}, u32[]{:S(2)}) collective-permute-start(f32[4096]{0:T(1024)S(1)} %maximum_select_fusion), channel_id=1, source_target_pairs={{0,8},{8,16},{16,24},{1,9},{9,17},{17,25},{2,10},{10,18},{18,26},{... | collective-permute-start | bytes 49160 | tf_op jit(solution)/shard_map/ppermute | solution.py:16
  65.0 2.5 %collective-permute-start.6 = (f32[512]{0:T(512)S(1)}, f32[512]{0:T(512)S(1)}, u32[]{:S(2)}, u32[]{:S(2)}) collective-permute-start(f32[512]{0:T(512)S(1)} %multiply_add_fusion.2), channel_id=1, source_target_pairs={{0,1},{1,0},{2,3},{3,2},{4,5},{5,4},{6,7},{7,6},{8,9},{9,8},{10,11... | collective-permute-start | bytes 6152 | tf_op jit(solution)/shard_map/ppermute | solution.py:86
  67.6 2.5 %collective-permute-start.7 = (f32[1024]{0:T(1024)S(1)}, f32[1024]{0:T(1024)S(1)}, u32[]{:S(2)}, u32[]{:S(2)}) collective-permute-start(f32[1024]{0:T(1024)S(1)} %maximum_select_fusion.9), channel_id=1, source_target_pairs={{0,2},{1,3},{2,0},{3,1},{4,6},{5,7},{6,4},{7,5},{8,10},{9,11},{10,... | collective-permute-start | bytes 12296 | tf_op jit(solution)/shard_map/ppermute | solution.py:86
  70.0 3.4 %collective-permute-start.8 = (f32[2048]{0:T(1024)S(1)}, f32[2048]{0:T(1024)S(1)}, u32[]{:S(2)}, u32[]{:S(2)}) collective-permute-start(f32[2048]{0:T(1024)S(1)} %maximum_select_fusion.5), channel_id=1, source_target_pairs={{0,4},{1,5},{2,6},{3,7},{4,0},{5,1},{6,2},{7,3},{8,12},{9,13},{10,... | collective-permute-start | bytes 24584 | tf_op jit(solution)/shard_map/ppermute | solution.py:86
  73.4 8.7 %collective-permute-start.9 = (f32[4096]{0:T(1024)S(1)}, f32[4096]{0:T(1024)S(1)}, u32[]{:S(2)}, u32[]{:S(2)}) collective-permute-start(f32[4096]{0:T(1024)S(1)} %maximum_select_fusion.1), channel_id=1, source_target_pairs={{8,0},{16,8},{24,16},{9,1},{17,9},{25,17},{10,2},{18,10},{26,18},{... | collective-permute-start | bytes 49160 | tf_op jit(solution)/shard_map/ppermute | solution.py:16
  86.4 2.5 %collective-permute-start.10 = (f32[512]{0:T(512)S(1)}, f32[512]{0:T(512)S(1)}, u32[]{:S(2)}, u32[]{:S(2)}) collective-permute-start(f32[512]{0:T(512)S(1)} %multiply_add_fusion.1), channel_id=1, source_target_pairs={{0,1},{1,0},{2,3},{3,2},{4,5},{5,4},{6,7},{7,6},{8,9},{9,8},{10,11... | collective-permute-start | bytes 6152 | tf_op jit(solution)/shard_map/ppermute | solution.py:86
  88.9 2.5 %collective-permute-start.11 = (f32[1024]{0:T(1024)S(1)}, f32[1024]{0:T(1024)S(1)}, u32[]{:S(2)}, u32[]{:S(2)}) collective-permute-start(f32[1024]{0:T(1024)S(1)} %maximum_select_fusion.10), channel_id=1, source_target_pairs={{0,2},{1,3},{2,0},{3,1},{4,6},{5,7},{6,4},{7,5},{8,10},{9,11},{10,... | collective-permute-start | bytes 12296 | tf_op jit(solution)/shard_map/ppermute | solution.py:86
  91.4 3.4 %collective-permute-start.12 = (f32[2048]{0:T(1024)S(1)}, f32[2048]{0:T(1024)S(1)}, u32[]{:S(2)}, u32[]{:S(2)}) collective-permute-start(f32[2048]{0:T(1024)S(1)} %maximum_select_fusion.6), channel_id=1, source_target_pairs={{0,4},{1,5},{2,6},{3,7},{4,0},{5,1},{6,2},{7,3},{8,12},{9,13},{10,... | collective-permute-start | bytes 24584 | tf_op jit(solution)/shard_map/ppermute | solution.py:86
  94.8 6.6 %collective-permute-start.13 = (f32[4096]{0:T(1024)S(1)}, f32[4096]{0:T(1024)S(1)}, u32[]{:S(2)}, u32[]{:S(2)}) collective-permute-start(f32[4096]{0:T(1024)S(1)} %maximum_select_fusion.2), channel_id=1, source_target_pairs={{0,8},{8,16},{16,24},{1,9},{9,17},{17,25},{2,10},{10,18},{18,26},{... | collective-permute-start | bytes 49160 | tf_op jit(solution)/shard_map/ppermute | solution.py:16
  105.7 2.5 %collective-permute-start.14 = (f32[512]{0:T(512)S(1)}, f32[512]{0:T(512)S(1)}, u32[]{:S(2)}, u32[]{:S(2)}) collective-permute-start(f32[512]{0:T(512)S(1)} %multiply_add_fusion), channel_id=1, source_target_pairs={{0,1},{1,0},{2,3},{3,2},{4,5},{5,4},{6,7},{7,6},{8,9},{9,8},{10,11... | collective-permute-start | bytes 6152 | tf_op jit(solution)/shard_map/ppermute | solution.py:86
  108.2 2.5 %collective-permute-start.15 = (f32[1024]{0:T(1024)S(1)}, f32[1024]{0:T(1024)S(1)}, u32[]{:S(2)}, u32[]{:S(2)}) collective-permute-start(f32[1024]{0:T(1024)S(1)} %maximum_select_fusion.11), channel_id=1, source_target_pairs={{0,2},{1,3},{2,0},{3,1},{4,6},{5,7},{6,4},{7,5},{8,10},{9,11},{10,... | collective-permute-start | bytes 12296 | tf_op jit(solution)/shard_map/ppermute | solution.py:86
  110.7 3.4 %collective-permute-start.16 = (f32[2048]{0:T(1024)S(1)}, f32[2048]{0:T(1024)S(1)}, u32[]{:S(2)}, u32[]{:S(2)}) collective-permute-start(f32[2048]{0:T(1024)S(1)} %maximum_select_fusion.7), channel_id=1, source_target_pairs={{0,4},{1,5},{2,6},{3,7},{4,0},{5,1},{6,2},{7,3},{8,12},{9,13},{10,... | collective-permute-start | bytes 24584 | tf_op jit(solution)/shard_map/ppermute | solution.py:86
  114.1 11.3 %collective-permute-start.17 = (f32[4096]{0:T(1024)S(1)}, f32[4096]{0:T(1024)S(1)}, u32[]{:S(2)}, u32[]{:S(2)}) collective-permute-start(f32[4096]{0:T(1024)S(1)} %maximum_select_fusion.3), channel_id=1, source_target_pairs={{8,0},{16,8},{24,16},{9,1},{17,9},{25,17},{10,2},{18,10},{26,18},{... | collective-permute-start | bytes 49160 | tf_op jit(solution)/shard_map/ppermute | solution.py:16
  129.8 3.5 %copy-start = (f32[1,64,512]{2,1,0:T(8,128)S(1)}, f32[1,64,512]{2,1,0:T(8,128)}, u32[]{:S(2)}) copy-start(f32[1,64,512]{2,1,0:T(8,128)} %param.16) | copy-start | bytes 393220
  129.8 3.5 %copy-start.1 = (f32[1,64,512]{2,1,0:T(8,128)S(1)}, f32[1,64,512]{2,1,0:T(8,128)}, u32[]{:S(2)}) copy-start(f32[1,64,512]{2,1,0:T(8,128)} %param.17) | copy-start | bytes 393220
